TPU v7x, 128 devices: a whole 4x4x4 slice. The times are simulated.
128 devices in a mesh: leaf: 64 (over y_hi, x, z, core), rhs: 2 (over y_lo).
Axes of the slice: x: 4, y: 4 (y_hi: 2, y_lo: 2; y = y_hi * 2 + y_lo), z: 4, core: 2. Of those that a mesh axis runs over, the one named last changes fastest.
Arguments:
- rhs: bfloat16 [524288, 512], P('leaf', 'rhs'), may hold values from -6 to 6
- source_basis: bfloat16 [4096, 128, 128], P('leaf', None, 'rhs'), may hold values from -0.5 to 0.5
- target_basis: bfloat16 [4096, 128, 128], P('leaf', None, 'rhs'), may hold values from -0.5 to 0.5
- near_blocks: bfloat16 [4096, 2, 128, 128], P('leaf', None, None, 'rhs'), may hold values from -0.375 to 0.375
- near_offsets: int32 [4096, 2], P('leaf'), may hold values from -2 to 2
- source_values: bfloat16 [3, 2048, 2, 2, 128, 128], P(None, 'leaf', None, None, 'rhs'), may hold values from -0.375 to 0.375
- source_scales: float32 [3, 2048, 2, 2, 128], P(None, 'leaf'), may hold values from 0.2 to 2
- target_values: bfloat16 [3, 2048, 2, 2, 128, 128], P(None, 'leaf', None, None, 'rhs'), may hold values from -0.375 to 0.375
- target_scales: float32 [3, 2048, 2, 2, 128], P(None, 'leaf'), may hold values from 0.2 to 2
Outputs:
- product: bfloat16 [524288, 512], P('leaf', 'rhs')
All inputs are finite; a program needn't handle non-finite values.
Results may differ from a plain program's by a relative error of at most 0.01.
Values may be sent and summed in bfloat16 or wider, within the bound.
A program may use at most 192 MiB of HBM per device.

v0:
```python
import jax
import jax.numpy as jnp
from jax import lax
from jax.sharding import PartitionSpec as P

REACH = 2
SRC_LEVELS = 3
TGT_LEVELS = 3


def padded_2(cells, sides, width):
    for axis, dim in sides:
        count = lax.axis_size(axis)
        ends = count - 1
        head = lax.slice_in_dim(cells, 0, width, axis=dim)
        tail = lax.slice_in_dim(cells, cells.shape[dim] - width, cells.shape[dim], axis=dim)
        cells = jnp.concatenate(
            [
                lax.ppermute(tail, axis, [(i, (i + 1) % count) for i in range(ends)]),
                cells,
                lax.ppermute(head, axis, [((i + 1) % count, i) for i in range(ends)]),
            ],
            axis=dim,
        )
    return cells


def dequantize(values, scales):
    return (values.astype(jnp.float32) * scales[..., None, :]).astype(jnp.bfloat16)


def butterfly_level(coefficients, blocks, bit_index):
    box_total, columns, rank = coefficients.shape
    outputs = blocks.shape[-2]
    low_span = 2**bit_index
    high_span = box_total // (2 * low_span)
    inputs = coefficients.reshape(high_span, 2, low_span, columns, rank)
    matrices = blocks.reshape(high_span, low_span, 2, 2, outputs, rank)
    mixed = jnp.einsum("hclnr,hlocsr->holns", inputs, matrices, preferred_element_type=jnp.float32)
    return mixed.reshape(box_total, columns, outputs).astype(jnp.bfloat16)


def apply_level(coefficients, scales, bit_index, gathered):
    return butterfly_level(coefficients, dequantize(gathered, scales), bit_index)


def on_device(
    rhs,
    source_basis,
    target_basis,
    near_blocks,
    near_offsets,
    source_values,
    source_scales,
    target_values,
    target_scales,
):
    box_count = source_basis.shape[0]
    box_rows = source_basis.shape[1]
    columns = rhs.shape[1]
    rhs_boxes = rhs.reshape(box_count, box_rows, columns)
    basis_in, basis_out, near_full = (
        lax.all_gather(source_basis, "rhs", axis=2, tiled=True),
        lax.all_gather(target_basis, "rhs", axis=2, tiled=True),
        lax.all_gather(near_blocks, "rhs", axis=3, tiled=True),
    )
    source_tables, target_tables = (
        lax.all_gather(source_values, "rhs", axis=4, tiled=True),
        lax.all_gather(target_values, "rhs", axis=4, tiled=True),
    )
    coefficients = jnp.einsum(
        "bmc,bmr->bcr", rhs_boxes, basis_in, preferred_element_type=jnp.float32
    ).astype(jnp.bfloat16)
    for level_index in range(SRC_LEVELS):
        coefficients = apply_level(
            coefficients, source_scales[level_index], level_index, source_tables[level_index]
        )
    padded = padded_2(rhs_boxes, (("leaf", 0),), REACH)
    source_index = jnp.arange(box_count, dtype=jnp.int32)[:, None] + REACH + near_offsets
    selected = jnp.take(padded, source_index, axis=0)
    near_field = jnp.einsum(
        "bkmn,bknc->bmc", near_full, selected, preferred_element_type=jnp.float32
    )
    row_coefficients = lax.all_to_all(coefficients, "leaf", split_axis=0, concat_axis=0, tiled=True)
    for level_index in range(TGT_LEVELS):
        row_coefficients = apply_level(
            row_coefficients, target_scales[level_index], level_index, target_tables[level_index]
        )
    far_field = jnp.einsum(
        "bmr,bcr->bmc", basis_out, row_coefficients, preferred_element_type=jnp.float32
    )
    return (far_field + near_field).astype(jnp.bfloat16).reshape(box_count * box_rows, columns)


def solution(mesh):
    placed = (
        P("leaf", "rhs"),
        P("leaf", None, "rhs"),
        P("leaf", None, "rhs"),
        P("leaf", None, None, "rhs"),
        P("leaf", None),
        P(None, "leaf", None, None, "rhs", None),
        P(None, "leaf", None, None, None),
        P(None, "leaf", None, None, "rhs", None),
        P(None, "leaf", None, None, None),
    )
    return jax.shard_map(
        on_device, mesh=mesh, in_specs=placed, out_specs=P("leaf", "rhs"), check_vma=False
    )
```

profile of v0, /device:TPU:30, one launch (start us, length us, event | category | flops | bytes accessed | tf_op | source)
XLA Modules:
  0.0 525.0 jit_solution(11540010097013420315)
XLA Ops:
  6.5 0.7 all-gather.10.cloned.1.call-update
  7.3 0.7 all-gather.8.cloned.1.call-update
  8.1 0.7 all-gather.6.cloned.1.call-update
  9.0 37.1 %all-gather.10.cloned.1.call-done = bf16[64,128,128]{1,2,0:T(8,128)(2,1)} async-done(((bf16[64,128,64]{1,2,0:T(8,128)(2,1)}), bf16[64,128,128]{1,2,0:T(8,128)(2,1)}) %all-gather.10.cloned.1.call-update) | async-done | bytes 2097168 | tf_op jit(solution)/shard_map/all_gather | solution.py:63
  46.0 6.2 %convolution_convert_fusion = bf16[64,256,128]{2,1,0:T(8,128)(2,1)} fusion(bf16[64,128,256]{2,1,0:T(8,128)(2,1)} %bitcast.118, bf16[64,128,128]{1,2,0:T(8,128)(2,1)} %all-gather.10.cloned.1.call-done), kind=kOutput, calls=%fused_computation.48 | convolution fusion | flops 538968064 | bytes 10485760 | tf_op jit(solution)/shard_map/bmc,bmr->bcr/dot_general | solution.py:71
  52.2 151.5 %all-gather.8.cloned.1.call-done = bf16[3,32,2,2,128,128]{5,4,3,2,1,0:T(8,128)(2,1)} async-done(((bf16[3,32,2,2,64,128]{5,4,3,2,1,0:T(8,128)(2,1)}), bf16[3,32,2,2,128,128]{5,4,3,2,1,0:T(8,128)(2,1)}) %all-gather.8.cloned.1.call-update) | async-done | bytes 12582928 | tf_op jit(solution)/shard_map/all_gather | solution.py:68
  203.7 5.4 %fusion.61 = (bf16[1,32,2,2,128,128]{5,4,3,2,1,0:T(8,128)(2,1)}, bf16[1,32,2,2,128,128]{5,4,3,2,1,0:T(8,128)(2,1)S(1)}) fusion(bf16[3,32,2,2,128,128]{5,4,3,2,1,0:T(8,128)(2,1)} %all-gather.8.cloned.1.call-done), kind=kLoop, calls=%fused_computation.57 | loop fusion | bytes 16777216 | tf_op jit(solution)/shard_map/slice | solution.py:76
  209.1 0.8 copy-done
  209.9 3.5 bitcast_convert_fusion.5
  213.4 3.6 fusion.10
  217.0 6.9 %copy.17 = bf16[16,2,2,256,128]{4,3,2,1,0:T(8,128)(2,1)} copy(bf16[16,2,2,256,128]{3,4,1,2,0:T(8,128)(2,1)} %fusion.10) | data formatting | bytes 8388608 | tf_op jit(solution)/shard_map/convert_element_type | solution.py:40
  223.9 7.4 %fusion.11 = bf16[8,2,4,256,128]{3,4,1,2,0:T(8,128)(2,1)} fusion(bf16[8,2,4,256,128,1]{4,3,2,1,0,5:T(8,128)(2,1)} %bitcast.123, bf16[8,4,2,2,128,128]{5,4,3,2,1,0:T(8,128)(2,1)} %bitcast.126, f32[8,4,2,2,128]{4,3,2,1,0:T(2,128)S(1)} %bitcast.133), kind=kOutput, calls=%fused_computation.26 | convolution fusion | flops 1082130432 | bytes 12648448 | tf_op jit(solution)/shard_map/hclnr,hlocsr->holns/dot_general | solution.py:39
  231.3 6.5 %copy.19 = bf16[8,2,4,256,128]{4,3,2,1,0:T(8,128)(2,1)} copy(bf16[8,2,4,256,128]{3,4,1,2,0:T(8,128)(2,1)} %fusion.11) | data formatting | bytes 8388608 | tf_op jit(solution)/shard_map/convert_element_type | solution.py:40
  237.8 10.9 %all-to-all-start = ((bf16[64,256,128]{2,1,0:T(8,128)(2,1)}), bf16[64,256,128]{2,1,0:T(8,128)(2,1)}, u32[]{:S(2)}, u32[]{:S(2)}) async-start(bf16[64,256,128]{2,1,0:T(8,128)(2,1)} %bitcast.121), calls=%async_computation | async-start | bytes 8388608 | tf_op jit(solution)/shard_map/all_to_all | solution.py:84
  249.4 0.5 all-gather.14.cloned.1.call-update
  249.9 1.0 fusion.62
  250.9 2.0 collective-permute-start
  253.0 5.8 %collective-permute-start.1 = (bf16[2,128,256]{2,1,0:T(8,128)(2,1)S(1)}, bf16[2,128,256]{2,1,0:T(8,128)(2,1)S(1)}, u32[]{:S(2)}, u32[]{:S(2)}) collective-permute-start(bf16[2,128,256]{2,1,0:T(8,128)(2,1)S(1)} %bitcast.129), channel_id=1, source_target_pairs={{2,0},{4,2},{6,4},{8,6},{10,8},{12,10},{14,12},{16,14},{18,16},{20... | collective-permute-start | bytes 393224 | tf_op jit(solution)/shard_map/ppermute | solution.py:21
  259.2 41.3 %collective-permute-done = bf16[2,128,256]{2,1,0:T(8,128)(2,1)S(1)} collective-permute-done((bf16[2,128,256]{2,1,0:T(8,128)(2,1)S(1)}, bf16[2,128,256]{2,1,0:T(8,128)(2,1)S(1)}, u32[]{:S(2)}, u32[]{:S(2)}) %collective-permute-start) | collective-permute-done | bytes 131104 | tf_op jit(solution)/shard_map/ppermute | solution.py:19
  300.5 4.0 pad_maximum_fusion
  304.4 8.8 %gather_fusion = bf16[128,128,256]{2,1,0:T(8,128)(2,1)} fusion(bf16[68,128,256]{2,1,0:T(8,128)(2,1)} %pad_maximum_fusion, s32[1024]{0:T(1024)S(1)} %pad_clamp_fusion), kind=kCustom, calls=%fused_computation | custom fusion | bytes 16777728 | tf_op jit(solution)/shard_map/jit(_take)/gather | solution.py:80
  313.3 95.8 %all-gather.6.cloned.1.call-done = bf16[3,32,2,2,128,128]{5,4,3,2,1,0:T(8,128)(2,1)} async-done(((bf16[3,32,2,2,64,128]{5,4,3,2,1,0:T(8,128)(2,1)}), bf16[3,32,2,2,128,128]{5,4,3,2,1,0:T(8,128)(2,1)}) %all-gather.6.cloned.1.call-update) | async-done | bytes 12582928 | tf_op jit(solution)/shard_map/all_gather | solution.py:69
  409.1 6.2 %fusion.60 = (bf16[1,32,2,2,128,128]{5,4,3,2,1,0:T(8,128)(2,1)}, bf16[1,32,2,2,128,128]{5,4,3,2,1,0:T(8,128)(2,1)}) fusion(bf16[3,32,2,2,128,128]{5,4,3,2,1,0:T(8,128)(2,1)} %all-gather.6.cloned.1.call-done), kind=kLoop, calls=%fused_computation.56 | loop fusion | bytes 16777216 | tf_op jit(solution)/shard_map/slice | solution.py:87
  415.3 4.9 bitcast_convert_fusion.2
  420.2 3.2 fusion.12
  423.4 6.5 %copy.21 = bf16[16,2,2,256,128]{4,3,2,1,0:T(8,128)(2,1)} copy(bf16[16,2,2,256,128]{3,4,1,2,0:T(8,128)(2,1)} %fusion.12) | data formatting | bytes 8388608 | tf_op jit(solution)/shard_map/convert_element_type | solution.py:40
  430.0 6.7 %fusion.13 = bf16[8,2,4,256,128]{3,4,1,2,0:T(8,128)(2,1)} fusion(bf16[8,2,4,256,128,1]{4,3,2,1,0,5:T(8,128)(2,1)} %bitcast.124, bf16[8,4,2,2,128,128]{5,4,3,2,1,0:T(8,128)(2,1)} %bitcast.125, f32[8,4,2,2,128]{4,3,2,1,0:T(2,128)S(1)} %bitcast.131), kind=kOutput, calls=%fused_computation.28 | convolution fusion | flops 1082130432 | bytes 12648448 | tf_op jit(solution)/shard_map/hclnr,hlocsr->holns/dot_general | solution.py:39
  436.7 6.4 %copy.23 = bf16[8,2,4,256,128]{4,3,2,1,0:T(8,128)(2,1)} copy(bf16[8,2,4,256,128]{3,4,1,2,0:T(8,128)(2,1)} %fusion.13) | data formatting | bytes 8388608 | tf_op jit(solution)/shard_map/convert_element_type | solution.py:40
  443.1 3.5 all-gather.12.cloned.1.call-done
  446.6 7.4 %fusion.65 = f32[64,256,128]{1,2,0:T(8,128)} fusion(bf16[64,256,128]{2,1,0:T(8,128)(2,1)} %bitcast.120, bf16[64,128,128]{1,2,0:T(8,128)(2,1)} %all-gather.12.cloned.1.call-done), kind=kOutput, calls=%fused_computation.61 | convolution fusion | flops 536870912 | bytes 14680064 | tf_op jit(solution)/shard_map/bmr,bcr->bmc/dot_general | solution.py:89
  454.1 54.3 %all-gather.14.cloned.1.call-done = bf16[64,2,128,128]{2,3,1,0:T(8,128)(2,1)} async-done(((bf16[64,2,128,64]{2,3,1,0:T(8,128)(2,1)}), bf16[64,2,128,128]{2,3,1,0:T(8,128)(2,1)}) %all-gather.14.cloned.1.call-update) | async-done | bytes 4194320 | tf_op jit(solution)/shard_map/all_gather | solution.py:65
  508.4 10.1 %fusion.6 = bf16[64,256,128]{1,2,0:T(8,128)(2,1)} fusion(f32[64,256,128]{1,2,0:T(8,128)} %fusion.65, bf16[64,2,128,128]{2,3,1,0:T(8,128)(2,1)} %all-gather.14.cloned.1.call-done, bf16[64,2,128,256]{3,2,1,0:T(8,128)(2,1)} %bitcast.117, pred[64,2]{1,0:T(8,128)(4,1)S(1)} %copy.24), kind=kOutput, calls=%fused_computation.14 | convolution fusion | flops 1082130432 | bytes 25165952 | tf_op jit(solution)/shard_map/bkmn,bknc->bmc/dot_general | solution.py:81
  (25 shorter events, 1.3 us)
Async XLA Ops:
  6.5 39.5 %all-gather.10.cloned.1.call-start = ((), (), s32[]{:S(2)}) async-start(), calls=%async_computation.3 | async-start | bytes 3145728 | tf_op jit(solution)/shard_map/all_gather | solution.py:63
  7.3 196.5 %all-gather.8.cloned.1.call-start = ((), (), s32[]{:S(2)}) async-start(), calls=%async_computation.2 | async-start | bytes 18874368 | tf_op jit(solution)/shard_map/all_gather | solution.py:68
  8.0 0.9 copy-start.2
  8.0 401.1 %all-gather.6.cloned.1.call-start = ((), (), s32[]{:S(2)}) async-start(), calls=%async_computation.1 | async-start | bytes 18874368 | tf_op jit(solution)/shard_map/all_gather | solution.py:69
  203.7 6.2 %copy-start = (bf16[64,256,128]{2,1,0:T(8,128)(2,1)S(1)}, bf16[64,256,128]{2,1,0:T(8,128)(2,1)}, u32[]{:S(2)}) copy-start(bf16[64,256,128]{2,1,0:T(8,128)(2,1)} %convolution_convert_fusion) | copy-start | bytes 12582916
  237.8 21.0 %copy-start.3 = (f32[3,32,2,2,128]{4,3,2,1,0:T(2,128)S(1)}, f32[3,32,2,2,128]{4,3,2,1,0:T(2,128)}, u32[]{:S(2)}) copy-start(f32[3,32,2,2,128]{4,3,2,1,0:T(2,128)} %param.17) | copy-start | bytes 589828
  237.8 21.0 %copy-start.4 = (s32[64,2]{0,1:T(2,128)S(1)}, s32[64,2]{0,1:T(2,128)}, u32[]{:S(2)}) copy-start(s32[64,2]{0,1:T(2,128)} %param.13) | copy-start | bytes 1540
  237.8 177.5 %all-to-all-start = ((bf16[64,256,128]{2,1,0:T(8,128)(2,1)}), bf16[64,256,128]{2,1,0:T(8,128)(2,1)}, u32[]{:S(2)}, u32[]{:S(2)}) async-start(bf16[64,256,128]{2,1,0:T(8,128)(2,1)} %bitcast.121), calls=%async_computation | async-start | bytes 8388608 | tf_op jit(solution)/shard_map/all_to_all | solution.py:84
  248.8 197.9 %all-gather.12.cloned.1.call-start = ((), (), s32[]{:S(2)}) async-start(), calls=%async_computation.4 | async-start | bytes 3145728 | tf_op jit(solution)/shard_map/all_gather | solution.py:64
  249.3 259.0 %all-gather.14.cloned.1.call-start = ((), (), s32[]{:S(2)}) async-start(), calls=%async_computation.5 | async-start | bytes 6291456 | tf_op jit(solution)/shard_map/all_gather | solution.py:65
  250.9 49.6 %collective-permute-start = (bf16[2,128,256]{2,1,0:T(8,128)(2,1)S(1)}, bf16[2,128,256]{2,1,0:T(8,128)(2,1)S(1)}, u32[]{:S(2)}, u32[]{:S(2)}) collective-permute-start(bf16[2,128,256]{2,1,0:T(8,128)(2,1)S(1)} %bitcast.130), channel_id=1, source_target_pairs={{0,2},{2,4},{4,6},{6,8},{8,10},{10,12},{12,14},{14,16},{16,18},{18... | collective-permute-start | bytes 393224 | tf_op jit(solution)/shard_map/ppermute | solution.py:19
  253.0 47.5 %collective-permute-start.1 = (bf16[2,128,256]{2,1,0:T(8,128)(2,1)S(1)}, bf16[2,128,256]{2,1,0:T(8,128)(2,1)S(1)}, u32[]{:S(2)}, u32[]{:S(2)}) collective-permute-start(bf16[2,128,256]{2,1,0:T(8,128)(2,1)S(1)} %bitcast.129), channel_id=1, source_target_pairs={{2,0},{4,2},{6,4},{8,6},{10,8},{12,10},{14,12},{16,14},{18,16},{20... | collective-permute-start | bytes 393224 | tf_op jit(solution)/shard_map/ppermute | solution.py:21
  415.3 4.9 copy-start.1
Sparse Core Ops, SparseCore 0:
  9.0 36.9 all-gather.9
  47.7 155.9 all-gather.7
  205.4 203.6 all-gather.5
  410.6 35.9 all-gather.11
  448.1 60.2 all-gather.13
where the time goes:
time: 528 us; the launch traced here: 525 us
  waiting for transfers between devices  387 us (73%)
  matrix products  53 us (10%)
  local copies, waits for them, and re-layouts  49.2 us (9%)
  starting transfers between devices  18.9 us (4%)
  between operations  13.3 us (3%)
    all_gather x1, waiting for transfers between devices, on_device(): lax.all_gather(source_values, 'rhs', axis=4, tiled=True)  152 us
    all_gather x1, waiting for transfers between devices, on_device(): lax.all_gather(target_values, 'rhs', axis=4, tiled=True)  95.8 us
    all_gather x1, waiting for transfers between devices, on_device(): lax.all_gather(near_blocks, 'rhs', axis=3, tiled=True)  54.3 us
    ppermute x1, waiting for transfers between devices, padded_2(): lax.ppermute(tail, axis, [(i, (i + 1) % count) for i in range(ends)])  41.3 us
    all_gather x1, waiting for transfers between devices, on_device(): lax.all_gather(source_basis, 'rhs', axis=2, tiled=True)  37.1 us
    dot_general x6, matrix products, butterfly_level(): jnp.einsum('hclnr,hlocsr->holns', inputs, matrices, preferred_element_typ...  29.3 us
    convert_element_type x4, local copies, waits for them, and re-layouts, butterfly_level(): return mixed.reshape(box_total, columns, outputs).astype(jnp.bfloat16)  26.4 us
    all_to_all x1, starting transfers between devices, on_device(): lax.all_to_all(coefficients, 'leaf', split_axis=0, concat_axis=0, tiled=T...  10.9 us
  transfers between devices with their start and end apart: 8, of which 6 were waited for; matrix products, arithmetic and copies ran while one was open for 18% of the time, Pallas kernels for 0%

commit v1 on v0

v1 whole, which is shorter than its diff:
```python
import jax
import jax.numpy as jnp
from jax import lax
from jax.experimental import pallas as pl
from jax.experimental.pallas import tpu as pltpu
from jax.sharding import PartitionSpec as P

MESH = pl.DeviceIdType.MESH
LEVELS = 3
STEPS = 4
GROUP = 8
HALF = 32
ROWS = 128
COLS = 256


def dot(a, b, contract_a=1):
    return lax.dot_general(
        a, b, (((contract_a,), (0,)), ((), ())), preferred_element_type=jnp.float32
    )


def kernel(
    rhs, basis_in, basis_out, near, offsets, values_in, scales_in, values_out, scales_out,
    out,
    x, w_in, w_out, w_near, v_in, v_out, s_in, s_out, z, y, o,
    load_sem, pair_send, pair_recv, halo_send, halo_recv, mix_send, mix_recv,
    back_send, back_recv, keep_sem,
):
    leaf = lax.axis_index("leaf")
    mine = lax.axis_index("rhs")
    other = 1 - mine
    side = leaf // HALF
    slot = leaf % HALF
    turn = (leaf // GROUP) % STEPS
    partner = (leaf, other)
    low, high = leaf > 0, leaf < 2 * HALF - 1
    rows_of = pl.multiple_of(mine * 64, 64)

    def copy_to(src, dst, send, recv, device):
        return pltpu.make_async_remote_copy(
            src_ref=src, dst_ref=dst, send_sem=send, recv_sem=recv,
            device_id=device, device_id_type=MESH,
        )

    def parts(step, owner):
        g = (turn + step) % STEPS
        h = (turn + STEPS - step) % STEPS
        box, row_box = owner * HALF + GROUP * g, owner * HALF + GROUP * h
        return (
            (rhs.at[pl.ds(box, 8)], x.at[pl.ds(2 + GROUP * g, 8), mine]),
            (basis_in.at[pl.ds(box, 8)], w_in.at[pl.ds(GROUP * g, 8), pl.ds(rows_of, 64)]),
            (
                values_in.at[:, pl.ds(2 * box, 16)],
                v_in.at[:, pl.ds(2 * GROUP * g, 16), pl.ds(rows_of, 64)],
            ),
            (
                values_out.at[:, pl.ds(2 * row_box, 16)],
                v_out.at[:, pl.ds(2 * GROUP * h, 16), pl.ds(rows_of, 64)],
            ),
            (
                basis_out.at[pl.ds(row_box, 8)],
                w_out.at[pl.ds(GROUP * h, 8), pl.ds(rows_of, 64)],
            ),
            (
                near.at[pl.ds(2 * row_box, 16)],
                w_near.at[pl.ds(2 * GROUP * h, 16), pl.ds(rows_of, 64)],
            ),
        )

    def inner(owner):
        return rhs.at[pl.ds(32 - 2 * owner, 2)], x.at[pl.ds(34 - 34 * owner, 2), mine]

    def load(step, part):
        src, dst = parts(step, mine)[part]
        return pltpu.make_async_copy(src, dst, load_sem.at[6 * step + part])

    def pair(step, part):
        src, dst = parts(step, other)[part]
        at = 6 * step + part
        return copy_to(src, dst, pair_send.at[at], pair_recv.at[at], partner)

    def pair_wait(step, part):
        src, dst = parts(step, mine)[part]
        return src, dst

    load_inner = pltpu.make_async_copy(*inner(mine), load_sem.at[24])
    load_scales = (
        pltpu.make_async_copy(scales_in.at[:, pl.ds(16 * mine, 16)], s_in, load_sem.at[25]),
        pltpu.make_async_copy(scales_out.at[:, pl.ds(16 * mine, 16)], s_out, load_sem.at[26]),
    )
    pair_inner = copy_to(*inner(other), pair_send.at[24], pair_recv.at[24], partner)
    halo_up = copy_to(
        rhs.at[pl.ds(62, 2)], x.at[pl.ds(0, 2), mine],
        halo_send.at[0], halo_recv.at[mine], (leaf + 1, 0),
    )
    halo_down = copy_to(
        rhs.at[pl.ds(0, 2)], x.at[pl.ds(34, 2), mine],
        halo_send.at[1], halo_recv.at[mine], (leaf - 1, 1),
    )

    def mix(j):
        return copy_to(
            z.at[j], y.at[slot], mix_send.at[j], mix_recv.at[slot], (mine * HALF + j, side)
        )

    def is_self(j):
        return (mine * HALF + j == leaf) & (side == mine)

    def back(b):
        return copy_to(
            o.at[other, b], out.at[mine * HALF + b], back_send.at[b], back_recv.at[b], partner
        )

    def keep(b):
        return pltpu.make_async_copy(o.at[mine, b], out.at[mine * HALF + b], keep_sem.at[b])

    for copy in load_scales:
        copy.start()
    for step in range(STEPS):
        for part in range(3):
            load(step, part).start()

    barrier = pltpu.get_barrier_semaphore()

    def greet(*device):
        pl.semaphore_signal(barrier, inc=1, device_id=device, device_id_type=MESH)

    greet(leaf, other)

    @pl.loop(0, HALF)
    def _(j):
        @pl.when(jnp.logical_not(is_self(j)))
        def _():
            greet(mine * HALF + j, side)

    @pl.when((mine == 0) & low)
    def _():
        greet(leaf - 1, 0)
        greet(leaf - 1, 1)

    @pl.when((mine == 1) & high)
    def _():
        greet(leaf + 1, 0)
        greet(leaf + 1, 1)

    pl.semaphore_wait(
        barrier,
        1 + HALF - (side == mine).astype(jnp.int32)
        + low.astype(jnp.int32) + high.astype(jnp.int32),
    )

    for step in range(STEPS):
        for part in range(3):
            pair(step, part).start()
    pair_inner.start()

    @pl.when(high)
    def _():
        halo_up.start()

    @pl.when(low)
    def _():
        halo_down.start()

    for step in range(STEPS):
        for part in range(3, 6):
            pair(step, part).start()
    for step in range(STEPS):
        for part in range(3, 6):
            load(step, part).start()
    load_inner.start()

    @pl.when((mine == 0) & jnp.logical_not(low))
    def _():
        x[0:2] = jnp.zeros((2, 2, ROWS, COLS), jnp.bfloat16)

    @pl.when((mine == 1) & jnp.logical_not(high))
    def _():
        x[34:36] = jnp.zeros((2, 2, ROWS, COLS), jnp.bfloat16)

    def arrived(step, part):
        load(step, part).wait()
        src, dst = parts(step, other)[part]
        at = 6 * step + part
        into = parts(step, mine)[part][1]
        copy_to(src, into, pair_send.at[at], pair_recv.at[at], partner).wait_recv()

    def levels(coeff, blocks, scales, g):
        for t in range(LEVELS):
            @pl.loop(0, 4)
            def _(q):
                i = GROUP * g + (q // 2**t) * 2 ** (t + 1) + q % 2**t
                j = i + 2**t
                pair_at = 4 * g + q

                def block(at_o, at_c):
                    return (
                        blocks[t, 4 * pair_at + 2 * at_o + at_c].astype(jnp.float32)
                        * scales[t, pair_at, at_o, at_c:at_c + 1, :]
                    ).astype(jnp.bfloat16)

                both = jnp.concatenate([coeff[i], coeff[j]], axis=0)
                first = dot(jnp.concatenate([block(0, 0), block(0, 1)], axis=1), both)
                second = dot(jnp.concatenate([block(1, 0), block(1, 1)], axis=1), both)
                coeff[i] = first.astype(jnp.bfloat16)
                coeff[j] = second.astype(jnp.bfloat16)

    for copy in load_scales:
        copy.wait()

    @pl.loop(0, STEPS)
    def _(step):
        g = (turn + step) % STEPS
        for part in range(3):
            arrived(step, part)

        @pl.loop(0, GROUP)
        def _(i):
            b = GROUP * g + i
            for c in range(2):
                z[b, :, COLS * c:COLS * (c + 1)] = dot(w_in[b], x[2 + b, c]).astype(jnp.bfloat16)

        levels(z, v_in, s_in, g)

        @pl.loop(0, GROUP)
        def _(i):
            j = GROUP * g + i

            @pl.when(is_self(j))
            def _():
                y[slot] = z[j]

            @pl.when(jnp.logical_not(is_self(j)))
            def _():
                mix(j).start()

    load_inner.wait()
    copy_to(
        inner(mine)[0], x.at[pl.ds(34 - 34 * mine, 2), other],
        pair_send.at[24], pair_recv.at[24], partner,
    ).wait_recv()

    @pl.when(((mine == 0) & low) | ((mine == 1) & high))
    def _():
        for c in range(2):
            copy_to(
                rhs.at[pl.ds(0, 2)], x.at[pl.ds(34 * mine, 2), c],
                halo_send.at[0], halo_recv.at[c], partner,
            ).wait_recv()

    @pl.loop(0, STEPS)
    def _(step):
        h = (turn + STEPS - step) % STEPS
        for part in range(3, 6):
            arrived(step, part)

        @pl.loop(0, GROUP)
        def _(i):
            d = GROUP * h + i

            @pl.when(jnp.logical_not(is_self(d)))
            def _():
                copy_to(
                    z.at[d], y.at[d], mix_send.at[d], mix_recv.at[d], partner
                ).wait_recv()

        levels(y, v_out, s_out, h)

        @pl.loop(0, GROUP)
        def _(i):
            b = GROUP * h + i
            first = b + 2 + offsets[0, HALF * mine + b]
            second = b + 2 + offsets[1, HALF * mine + b]
            left = jnp.concatenate([w_out[b], w_near[2 * b], w_near[2 * b + 1]], axis=0)
            for c in range(2):
                right = jnp.concatenate(
                    [y[b, :, COLS * c:COLS * (c + 1)], x[first, c], x[second, c]], axis=0
                )
                o[c, b] = dot(left, right, 0).astype(jnp.bfloat16)
            back(b).start()
            keep(b).start()

    for step in range(STEPS):
        for part in range(6):
            pair(step, part).wait_send()
    pair_inner.wait_send()

    @pl.when(high)
    def _():
        halo_up.wait_send()

    @pl.when(low)
    def _():
        halo_down.wait_send()

    @pl.loop(0, HALF)
    def _(j):
        @pl.when(jnp.logical_not(is_self(j)))
        def _():
            mix(j).wait_send()

        keep(j).wait()
        back(j).wait_send()
        copy_to(
            o.at[other, j], out.at[other * HALF + j], back_send.at[j], back_recv.at[j], partner
        ).wait_recv()


def on_device(
    rhs, source_basis, target_basis, near_blocks, near_offsets,
    source_values, source_scales, target_values, target_scales,
):
    boxes = source_basis.shape[0]
    anywhere = pl.BlockSpec(memory_space=pl.ANY)
    bf16, f32 = jnp.bfloat16, jnp.float32
    product = pl.pallas_call(
        kernel,
        out_shape=jax.ShapeDtypeStruct((boxes, ROWS, COLS), bf16),
        in_specs=[anywhere] * 4 + [pl.BlockSpec(memory_space=pltpu.SMEM)] + [anywhere] * 4,
        out_specs=anywhere,
        scratch_shapes=[
            pltpu.VMEM((HALF + 4, 2, ROWS, COLS), bf16),
            pltpu.VMEM((HALF, 128, 128), bf16),
            pltpu.VMEM((HALF, 128, 128), bf16),
            pltpu.VMEM((2 * HALF, 128, 128), bf16),
            pltpu.VMEM((LEVELS, 2 * HALF, 128, 128), bf16),
            pltpu.VMEM((LEVELS, 2 * HALF, 128, 128), bf16),
            pltpu.VMEM((LEVELS, HALF // 2, 2, 2, 128), f32),
            pltpu.VMEM((LEVELS, HALF // 2, 2, 2, 128), f32),
            pltpu.VMEM((HALF, 128, 2 * COLS), bf16),
            pltpu.VMEM((HALF, 128, 2 * COLS), bf16),
            pltpu.VMEM((2, HALF, ROWS, COLS), bf16),
            pltpu.SemaphoreType.DMA((27,)),
            pltpu.SemaphoreType.DMA((25,)),
            pltpu.SemaphoreType.DMA((25,)),
            pltpu.SemaphoreType.DMA((2,)),
            pltpu.SemaphoreType.DMA((2,)),
            pltpu.SemaphoreType.DMA((HALF,)),
            pltpu.SemaphoreType.DMA((HALF,)),
            pltpu.SemaphoreType.DMA((HALF,)),
            pltpu.SemaphoreType.DMA((HALF,)),
            pltpu.SemaphoreType.DMA((HALF,)),
        ],
        compiler_params=pltpu.CompilerParams(
            collective_id=0, has_side_effects=True, vmem_limit_bytes=56 << 20
        ),
        name="butterfly",
    )(
        rhs.reshape(boxes, ROWS, COLS),
        jnp.swapaxes(source_basis, 1, 2),
        jnp.swapaxes(target_basis, 1, 2),
        jnp.swapaxes(near_blocks, 2, 3).reshape(2 * boxes, 64, 128),
        near_offsets.T,
        source_values.reshape(LEVELS, 2 * boxes, 64, 128),
        source_scales,
        target_values.reshape(LEVELS, 2 * boxes, 64, 128),
        target_scales,
    )
    return product.reshape(boxes * ROWS, COLS)


def solution(mesh):
    placed = (
        P("leaf", "rhs"),
        P("leaf", None, "rhs"),
        P("leaf", None, "rhs"),
        P("leaf", None, None, "rhs"),
        P("leaf", None),
        P(None, "leaf", None, None, "rhs", None),
        P(None, "leaf", None, None, None),
        P(None, "leaf", None, None, "rhs", None),
        P(None, "leaf", None, None, None),
    )
    return jax.shard_map(
        on_device, mesh=mesh, in_specs=placed, out_specs=P("leaf", "rhs"), check_vma=False
    )
```

time: 528 us -> 294 us (0.56)
  waiting for transfers between devices: 387 us -> 0 us
  Pallas kernels: 0 us -> 286 us
  matrix products: 53 us -> 0 us
  local copies, waits for them, and re-layouts: 49.2 us -> 4.47 us
  starting transfers between devices: 18.9 us -> 0 us
  between operations: 13.3 us -> 0.01 us
    all_gather x5 -> x0, waiting for transfers between devices: 342 us -> none  [the longest x1 152 us: on_device(): lax.all_gather(source_values, 'rhs', axis=4, tiled=True)]
    pallas_call x0 -> x1, Pallas kernels: none -> 286 us  [on_device(): pl.pallas_call(kernel, out_shape=jax.ShapeDtypeStruct((boxes, ROWS, COLS)...]
    dot_general x9 -> x0, matrix products: 53 us -> none  [the longest x6 29.3 us: butterfly_level(): jnp.einsum('hclnr,hlocsr->holns', inputs, matrices, preferred_element_typ...]
    ppermute x2 -> x0, waiting for transfers between devices: 41.3 us -> none  [the longest x1 41.3 us: padded_2(): lax.ppermute(tail, axis, [(i, (i + 1) % count) for i in range(ends)])]
    convert_element_type x4 -> x0, local copies, waits for them, and re-layouts: 26.4 us -> none  [butterfly_level(): return mixed.reshape(box_total, columns, outputs).astype(jnp.bfloat16)]
    slice x5 -> x0, local copies, waits for them, and re-layouts: 12.6 us -> none  [the longest x1 6.22 us: on_device(): target_tables[level_index]]
    all_to_all x1 -> x0, starting transfers between devices: 10.9 us -> none  [on_device(): lax.all_to_all(coefficients, 'leaf', split_axis=0, concat_axis=0, tiled=T...]
    gather x1 -> x0, local copies, waits for them, and re-layouts: 8.82 us -> none  [on_device(): selected = jnp.take(padded, source_index, axis=0)]
  transfers between devices with their start and end apart: 8 -> 0, of which waited for: 6 -> 0; matrix products, arithmetic and copies ran while one was open for 18% -> 0% of each run, Pallas kernels for 0% -> 0%
where the time goes in v1:
time: 294 us; the launch traced here: 291 us
  Pallas kernels  286 us (97%)
  local copies, waits for them, and re-layouts  4.47 us (2%)
    pallas_call x1, Pallas kernels, on_device(): pl.pallas_call(kernel, out_shape=jax.ShapeDtypeStruct((boxes, ROWS, COLS)...  286 us

profile of v1, /device:TPU:30, one launch (start us, length us, event | category | flops | bytes accessed | tf_op | source)
XLA Modules:
  0.0 290.5 jit_solution(9523391420261713322)
XLA Ops:
  0.0 286.1 %butterfly.1 = bf16[64,128,256]{2,1,0:T(8,128)(2,1)} custom-call(bf16[64,128,256]{2,1,0:T(8,128)(2,1)} %bitcast.13, bf16[64,64,128]{2,1,0:T(8,128)(2,1)} %bitcast.15, bf16[64,64,128]{2,1,0:T(8,128)(2,1)} %bitcast.16, bf16[128,64,128]{2,1,0:T(8,128)(2,1)} %bitcast.14, s32[2,64]{1,0:T(2,128)} %bitcast.17, bf16[3,128,64,128]{3,2,1,0:T(8,128)(2,1)} %bitcast.11, ...), custom_call_target="tpu_custom_call" | custom-call | tf_op jit(solution)/shard_map/butterfly/pallas_call | solution.py:317
  286.1 4.5 %copy.11 = bf16[8192,256]{1,0:T(8,128)(2,1)} copy(bf16[8192,256]{1,0:T(8,128)(2,1)} %bitcast.10) | data formatting | bytes 8388608

commit v2 on v1

v2 whole, which is shorter than its diff:
```python
import jax
import jax.numpy as jnp
from jax import lax
from jax.experimental import pallas as pl
from jax.experimental.pallas import tpu as pltpu
from jax.sharding import PartitionSpec as P

MESH = pl.DeviceIdType.MESH
LEVELS = 3
STEPS = 4
GROUP = 8
HALF = 32
ROWS = 128
COLS = 256


def dot(a, b, contract_a=1):
    return lax.dot_general(
        a, b, (((contract_a,), (0,)), ((), ())), preferred_element_type=jnp.float32
    )


def kernel(
    rhs, basis_in, basis_out, near, offsets, values_in, scales_in, values_out, scales_out,
    out,
    x, x_other, w_in, w_out, w_near, w_edge, v_in, v_out, s_in, s_out, z, y, o, edge,
    load_sem, pair_send, pair_recv, halo_send, halo_recv, mix_send, mix_recv,
    back_send, back_recv, known,
):
    leaf = lax.axis_index("leaf")
    mine = lax.axis_index("rhs")
    other = 1 - mine
    side = leaf // HALF
    slot = leaf % HALF
    turn = (leaf // GROUP) % STEPS
    partner = (leaf, other)
    low, high = leaf > 0, leaf < 2 * HALF - 1
    half_rows = pl.ds(pl.multiple_of(mine * 64, 64), 64)
    place = (2 * side + mine, slot // 8, slot // 2 % 4, slot % 2)

    def around(axis, by):
        spot = list(place)
        spot[axis] = (spot[axis] + by) % (2 if axis == 3 else 4)
        return (
            (spot[0] // 2) * HALF + spot[1] * 8 + spot[2] * 2 + spot[3], spot[0] % 2
        )

    def signal(sem, device):
        pl.semaphore_signal(sem, inc=1, device_id=device, device_id_type=MESH)

    def copy_to(src, dst, send, recv, device):
        return pltpu.make_async_remote_copy(
            src_ref=src, dst_ref=dst, send_sem=send, recv_sem=recv,
            device_id=device, device_id_type=MESH,
        )

    def parts(step, owner, columns):
        g = (turn + step) % STEPS
        h = (turn + STEPS - step) % STEPS
        box, row_box = owner * HALF + GROUP * g, owner * HALF + GROUP * h
        return (
            (rhs.at[pl.ds(box, 8)], columns(box, GROUP * g)),
            (basis_in.at[pl.ds(box, 8)], w_in.at[pl.ds(GROUP * g, 8), half_rows]),
            (
                values_in.at[:, pl.ds(2 * box, 16)],
                v_in.at[:, pl.ds(2 * GROUP * g, 16), half_rows],
            ),
            (
                values_out.at[:, pl.ds(2 * row_box, 16)],
                v_out.at[:, pl.ds(2 * GROUP * h, 16), half_rows],
            ),
            (basis_out.at[pl.ds(row_box, 8)], w_out.at[pl.ds(GROUP * h, 8), half_rows]),
            (
                near.at[pl.ds(2 * row_box, 16)],
                w_near.at[pl.ds(2 * GROUP * h, 16), half_rows],
            ),
        )

    def load(step, part):
        src, dst = parts(step, mine, lambda box, at: x.at[pl.ds(2 + box, 8)])[part]
        return pltpu.make_async_copy(src, dst, load_sem.at[6 * step + part])

    def pair(step, part, owner=other):
        src, dst = parts(step, owner, lambda box, at: x_other.at[pl.ds(at, 8)])[part]
        at = 6 * step + part
        return copy_to(src, dst, pair_send.at[at], pair_recv.at[at], partner)

    def edges(at, owner):
        first = 2 * (HALF * owner + 30 * at)
        return near.at[pl.ds(first, 4)], w_edge.at[pl.ds(4 * at, 4), half_rows]

    load_rest = [
        pltpu.make_async_copy(*edges(at, other), load_sem.at[24 + at]) for at in range(2)
    ] + [
        pltpu.make_async_copy(
            rhs.at[pl.ds(HALF * other, HALF)], x.at[pl.ds(2 + HALF * other, HALF)],
            load_sem.at[26],
        )
    ]
    load_scales = [
        pltpu.make_async_copy(scales_in.at[:, pl.ds(16 * mine, 16)], s_in, load_sem.at[27]),
        pltpu.make_async_copy(scales_out.at[:, pl.ds(16 * mine, 16)], s_out, load_sem.at[28]),
    ]
    pair_edges = [
        copy_to(*edges(at, mine), pair_send.at[24 + at], pair_recv.at[24 + at], partner)
        for at in range(2)
    ]
    halo_up = copy_to(
        rhs.at[pl.ds(62, 2)], x.at[pl.ds(0, 2)],
        halo_send.at[0], halo_recv.at[0], (leaf + 1, mine),
    )
    halo_down = copy_to(
        rhs.at[pl.ds(0, 2)], x.at[pl.ds(66, 2)],
        halo_send.at[1], halo_recv.at[1], (leaf - 1, mine),
    )

    def mix(j):
        return copy_to(
            z.at[j], y.at[slot], mix_send.at[j], mix_recv.at[slot], (mine * HALF + j, side)
        )

    def is_self(j):
        return (mine * HALF + j == leaf) & (side == mine)

    def on_edge(b):
        return (b < 2) | (b >= HALF - 2)

    def back(b, owner=mine):
        return copy_to(
            o.at[b], out.at[owner * HALF + b], back_send.at[b], back_recv.at[b], partner
        )

    def back_edge(b):
        return copy_to(
            o.at[b], edge.at[b % 28], back_send.at[b], back_recv.at[b], partner
        )

    barrier = pltpu.get_barrier_semaphore()
    beside = [around(axis, by) for axis in range(3) for by in (1, 3)] + [around(3, 1)]
    for device in beside:
        signal(barrier, device)
    for step in range(STEPS):
        for part in range(3):
            load(step, part).start()
    for copy in load_scales:
        copy.start()
    pl.semaphore_wait(barrier, len(beside))

    for step in range(STEPS):
        for part in range(3):
            pair(step, part).start()
    for step in range(STEPS):
        for part in range(3, 6):
            pair(step, part).start()
    for copy in pair_edges:
        copy.start()

    spread = ((1, (1,)), (2, (1, 3)), (2, (1,)), (3, (1,)), (0, (1, 3)), (0, (1,)))
    for stage, (axis, hops) in enumerate(spread):
        for by in hops:
            signal(known.at[stage], around(axis, by))
        pl.semaphore_wait(known.at[stage], len(hops))

    @pl.when(high)
    def _():
        halo_up.start()

    @pl.when(low)
    def _():
        halo_down.start()

    for step in range(STEPS):
        for part in range(3, 6):
            load(step, part).start()
    for copy in load_rest:
        copy.start()

    @pl.when(jnp.logical_not(low))
    def _():
        x[0:2] = jnp.zeros((2, ROWS, COLS), jnp.bfloat16)

    @pl.when(jnp.logical_not(high))
    def _():
        x[66:68] = jnp.zeros((2, ROWS, COLS), jnp.bfloat16)

    def arrived(step, part):
        load(step, part).wait()
        pair(step, part, mine).wait_recv()

    def levels(coeff, blocks, scales, g):
        for t in range(LEVELS):
            @pl.loop(0, 4)
            def _(q):
                i = GROUP * g + (q // 2**t) * 2 ** (t + 1) + q % 2**t
                j = i + 2**t
                pair_at = 4 * g + q

                def block(at_o, at_c):
                    return (
                        blocks[t, 4 * pair_at + 2 * at_o + at_c].astype(jnp.float32)
                        * scales[t, pair_at, at_o, at_c:at_c + 1, :]
                    ).astype(jnp.bfloat16)

                above = jnp.concatenate([block(0, 0), block(0, 1)], axis=1)
                below = jnp.concatenate([block(1, 0), block(1, 1)], axis=1)
                for c in range(2):
                    both = jnp.concatenate([coeff[i, c], coeff[j, c]], axis=0)
                    first, second = dot(above, both), dot(below, both)
                    coeff[i, c] = first.astype(jnp.bfloat16)
                    coeff[j, c] = second.astype(jnp.bfloat16)

    for copy in load_scales:
        copy.wait()

    @pl.loop(0, STEPS)
    def _(step):
        g = (turn + step) % STEPS
        for part in range(3):
            arrived(step, part)

        @pl.loop(0, GROUP)
        def _(i):
            b = GROUP * g + i
            z[b, mine] = dot(w_in[b], x[2 + HALF * mine + b]).astype(jnp.bfloat16)
            z[b, other] = dot(w_in[b], x_other[b]).astype(jnp.bfloat16)

        levels(z, v_in, s_in, g)

        @pl.loop(0, GROUP)
        def _(i):
            j = GROUP * g + i

            @pl.when(is_self(j))
            def _():
                y[slot] = z[j]

            @pl.when(jnp.logical_not(is_self(j)))
            def _():
                mix(j).start()

    for copy in load_rest:
        copy.wait()

    @pl.when(low)
    def _():
        halo_up.wait_recv()

    @pl.when(high)
    def _():
        halo_down.wait_recv()

    @pl.loop(0, STEPS)
    def _(step):
        h = (turn + STEPS - step) % STEPS
        for part in range(3, 6):
            arrived(step, part)

        @pl.loop(0, GROUP)
        def _(i):
            d = GROUP * h + i

            @pl.when(jnp.logical_not(is_self(d)))
            def _():
                copy_to(
                    z.at[d], y.at[d], mix_send.at[d], mix_recv.at[d], partner
                ).wait_recv()

        levels(y, v_out, s_out, h)

        @pl.loop(0, GROUP)
        def _(i):
            b = GROUP * h + (i + 6) % GROUP
            row = HALF * mine + b
            first, second = offsets[0, row], offsets[1, row]

            @pl.when(on_edge(b))
            def _():
                o[b] = dot(w_out[b], y[b, other], 0).astype(jnp.bfloat16)
                back_edge(b).start()

            left = jnp.concatenate([w_out[b], w_near[2 * b], w_near[2 * b + 1]], axis=0)

            @pl.when(jnp.logical_not(on_edge(b)))
            def _():
                right = jnp.concatenate(
                    [y[b, other], x_other[b + first], x_other[b + second]], axis=0
                )
                o[b] = dot(left, right, 0).astype(jnp.bfloat16)
                back(b).start()

            right = jnp.concatenate(
                [y[b, mine], x[2 + row + first], x[2 + row + second]], axis=0
            )
            out[row] = dot(left, right, 0).astype(jnp.bfloat16)

    for copy in pair_edges:
        copy.wait_recv()

    @pl.loop(0, 4)
    def _(e):
        b = e + 28 * (e // 2)
        row = HALF * other + b
        left = jnp.concatenate([w_edge[2 * e], w_edge[2 * e + 1]], axis=0)
        right = jnp.concatenate(
            [x[2 + row + offsets[0, row]], x[2 + row + offsets[1, row]]], axis=0
        )
        add = dot(left, right, 0)
        back_edge(b).wait_recv()
        out[row] = (edge[e].astype(jnp.float32) + add).astype(jnp.bfloat16)

    for step in range(STEPS):
        for part in range(6):
            pair(step, part).wait_send()
    for copy in pair_edges:
        copy.wait_send()

    @pl.when(high)
    def _():
        halo_up.wait_send()

    @pl.when(low)
    def _():
        halo_down.wait_send()

    @pl.loop(0, HALF)
    def _(j):
        @pl.when(jnp.logical_not(is_self(j)))
        def _():
            mix(j).wait_send()

        back(j).wait_send()

        @pl.when(jnp.logical_not(on_edge(j)))
        def _():
            back(j, other).wait_recv()


def on_device(
    rhs, source_basis, target_basis, near_blocks, near_offsets,
    source_values, source_scales, target_values, target_scales,
):
    boxes = source_basis.shape[0]
    anywhere = pl.BlockSpec(memory_space=pltpu.HBM)
    bf16, f32 = jnp.bfloat16, jnp.float32
    product = pl.pallas_call(
        kernel,
        out_shape=pltpu.VMEM((boxes, ROWS, COLS), bf16),
        in_specs=[anywhere] * 4 + [pl.BlockSpec(memory_space=pltpu.SMEM)] + [anywhere] * 4,
        out_specs=pl.BlockSpec(memory_space=pltpu.VMEM),
        scratch_shapes=[
            pltpu.VMEM((2 * HALF + 4, ROWS, COLS), bf16),
            pltpu.VMEM((HALF, ROWS, COLS), bf16),
            pltpu.VMEM((HALF, 128, 128), bf16),
            pltpu.VMEM((HALF, 128, 128), bf16),
            pltpu.VMEM((2 * HALF, 128, 128), bf16),
            pltpu.VMEM((8, 128, 128), bf16),
            pltpu.VMEM((LEVELS, 2 * HALF, 128, 128), bf16),
            pltpu.VMEM((LEVELS, 2 * HALF, 128, 128), bf16),
            pltpu.VMEM((LEVELS, HALF // 2, 2, 2, 128), f32),
            pltpu.VMEM((LEVELS, HALF // 2, 2, 2, 128), f32),
            pltpu.VMEM((HALF, 2, 128, COLS), bf16),
            pltpu.VMEM((HALF, 2, 128, COLS), bf16),
            pltpu.VMEM((HALF, ROWS, COLS), bf16),
            pltpu.VMEM((4, ROWS, COLS), bf16),
            pltpu.SemaphoreType.DMA((29,)),
            pltpu.SemaphoreType.DMA((26,)),
            pltpu.SemaphoreType.DMA((26,)),
            pltpu.SemaphoreType.DMA((2,)),
            pltpu.SemaphoreType.DMA((2,)),
            pltpu.SemaphoreType.DMA((HALF,)),
            pltpu.SemaphoreType.DMA((HALF,)),
            pltpu.SemaphoreType.DMA((HALF,)),
            pltpu.SemaphoreType.DMA((HALF,)),
            pltpu.SemaphoreType.REGULAR((6,)),
        ],
        compiler_params=pltpu.CompilerParams(
            collective_id=0, has_side_effects=True, vmem_limit_bytes=58 << 20
        ),
        name="butterfly",
    )(
        rhs.reshape(boxes, ROWS, COLS),
        jnp.swapaxes(source_basis, 1, 2),
        jnp.swapaxes(target_basis, 1, 2),
        jnp.swapaxes(near_blocks, 2, 3).reshape(2 * boxes, 64, 128),
        near_offsets.T,
        source_values.reshape(LEVELS, 2 * boxes, 64, 128),
        source_scales,
        target_values.reshape(LEVELS, 2 * boxes, 64, 128),
        target_scales,
    )
    return product.reshape(boxes * ROWS, COLS)


def solution(mesh):
    placed = (
        P("leaf", "rhs"),
        P("leaf", None, "rhs"),
        P("leaf", None, "rhs"),
        P("leaf", None, None, "rhs"),
        P("leaf", None),
        P(None, "leaf", None, None, "rhs", None),
        P(None, "leaf", None, None, None),
        P(None, "leaf", None, None, "rhs", None),
        P(None, "leaf", None, None, None),
    )
    return jax.shard_map(
        on_device, mesh=mesh, in_specs=placed, out_specs=P("leaf", "rhs"), check_vma=False
    )
```

time: 294 us -> 285 us (0.969)
  Pallas kernels: 286 us -> 282 us
    pallas_call x1, Pallas kernels: 286 us -> 282 us  [on_device(): pl.pallas_call(kernel, out_shape=pltpu.VMEM((boxes, ROWS, COLS), bf16), i...]
where the time goes in v2:
time: 285 us; the launch traced here: 284 us
  Pallas kernels  282 us (99%)
    pallas_call x1, Pallas kernels, on_device(): pl.pallas_call(kernel, out_shape=pltpu.VMEM((boxes, ROWS, COLS), bf16), i...  282 us

profile of v2, /device:TPU:30, one launch (start us, length us, event | category | flops | bytes accessed | tf_op | source)
XLA Modules:
  0.0 284.4 jit_solution(6676049349961337103)
XLA Ops:
  0.0 282.3 %butterfly.1 = bf16[64,128,256]{2,1,0:T(8,128)(2,1)S(1)} custom-call(bf16[64,128,256]{2,1,0:T(8,128)(2,1)} %bitcast.13, bf16[64,64,128]{2,1,0:T(8,128)(2,1)} %bitcast.15, bf16[64,64,128]{2,1,0:T(8,128)(2,1)} %bitcast.16, bf16[128,64,128]{2,1,0:T(8,128)(2,1)} %bitcast.14, s32[2,64]{1,0:T(2,128)} %bitcast.17, bf16[3,128,64,128]{3,2,1,0:T(8,128)(2,1)} %bitcast.11, ...), custom_call_target="tpu_custom_call" | custom-call | tf_op jit(solution)/shard_map/butterfly/pallas_call | solution.py:345
  282.3 2.0 copy.11

commit v3 on v2

--- a/solution.py
+++ b/solution.py
@@ -21,9 +21,9 @@
 
 
 def kernel(
-    rhs, basis_in, basis_out, near, offsets, values_in, scales_in, values_out, scales_out,
+    rhs, basis_in, basis_out, near, near_offsets, values_in, scales_in, values_out, scales_out,
     out,
-    x, x_other, w_in, w_out, w_near, w_edge, v_in, v_out, s_in, s_out, z, y, o, edge,
+    x, x_other, w_in, w_out, w_near, w_edge, v_in, v_out, s_in, s_out, z, y, o, edge, offsets,
     load_sem, pair_send, pair_recv, halo_send, halo_recv, mix_send, mix_recv,
     back_send, back_recv, known,
 ):
@@ -100,6 +100,7 @@
     load_scales = [
         pltpu.make_async_copy(scales_in.at[:, pl.ds(16 * mine, 16)], s_in, load_sem.at[27]),
         pltpu.make_async_copy(scales_out.at[:, pl.ds(16 * mine, 16)], s_out, load_sem.at[28]),
+        pltpu.make_async_copy(near_offsets, offsets, load_sem.at[29]),
     ]
     pair_edges = [
         copy_to(*edges(at, mine), pair_send.at[24 + at], pair_recv.at[24 + at], partner)
@@ -136,15 +137,26 @@
         )
 
     barrier = pltpu.get_barrier_semaphore()
-    beside = [around(axis, by) for axis in range(3) for by in (1, 3)] + [around(3, 1)]
-    for device in beside:
-        signal(barrier, device)
-    for step in range(STEPS):
-        for part in range(3):
-            load(step, part).start()
-    for copy in load_scales:
-        copy.start()
-    pl.semaphore_wait(barrier, len(beside))
+    core = place[3]
+    hub = (mine == 0) & (core == 0)
+    beside_hub = (mine == 1) & (core == 0)
+    lead = (mine == 0) & (core == 1)
+
+    @pl.when(jnp.logical_not(beside_hub))
+    def _():
+        signal(barrier, partner)
+
+    @pl.when(jnp.logical_not(hub))
+    def _():
+        pl.semaphore_wait(barrier, 1)
+
+    @pl.when(beside_hub)
+    def _():
+        signal(known.at[0], partner)
+
+    @pl.when(hub)
+    def _():
+        pl.semaphore_wait(known.at[0], 1)
 
     for step in range(STEPS):
         for part in range(3):
@@ -154,26 +166,48 @@
             pair(step, part).start()
     for copy in pair_edges:
         copy.start()
-
-    spread = ((1, (1,)), (2, (1, 3)), (2, (1,)), (3, (1,)), (0, (1, 3)), (0, (1,)))
-    for stage, (axis, hops) in enumerate(spread):
-        for by in hops:
-            signal(known.at[stage], around(axis, by))
-        pl.semaphore_wait(known.at[stage], len(hops))
-
-    @pl.when(high)
-    def _():
-        halo_up.start()
-
-    @pl.when(low)
-    def _():
-        halo_down.start()
-
+    for step in range(STEPS):
+        for part in range(3):
+            load(step, part).start()
+    for copy in load_scales:
+        copy.start()
     for step in range(STEPS):
         for part in range(3, 6):
             load(step, part).start()
     for copy in load_rest:
         copy.start()
+
+    @pl.when(lead)
+    def _():
+        signal(barrier, around(3, 1))
+        pl.semaphore_wait(known.at[6], 1)
+        signal(known.at[7], partner)
+
+    @pl.when(hub)
+    def _():
+        sides = [around(axis, by) for axis in (1, 2) for by in (1, 3)] + [around(0, 2)]
+        for device in sides:
+            signal(barrier, device)
+        pl.semaphore_wait(barrier, len(sides) + 1)
+        spread = ((1, (1, 3)), (1, (1,)), (2, (1, 3)), (2, (1,)), (0, (2,)))
+        for stage, (axis, hops) in enumerate(spread):
+            for by in hops:
+                signal(known.at[1 + stage], around(axis, by))
+            pl.semaphore_wait(known.at[1 + stage], len(hops))
+        signal(known.at[6], around(3, 1))
+        signal(known.at[7], partner)
+
+    @pl.when(mine == 1)
+    def _():
+        pl.semaphore_wait(known.at[7], 1)
+
+    @pl.when(high)
+    def _():
+        halo_up.start()
+
+    @pl.when(low)
+    def _():
+        halo_down.start()
 
     @pl.when(jnp.logical_not(low))
     def _():
@@ -345,7 +379,7 @@
     product = pl.pallas_call(
         kernel,
         out_shape=pltpu.VMEM((boxes, ROWS, COLS), bf16),
-        in_specs=[anywhere] * 4 + [pl.BlockSpec(memory_space=pltpu.SMEM)] + [anywhere] * 4,
+        in_specs=[anywhere] * 9,
         out_specs=pl.BlockSpec(memory_space=pltpu.VMEM),
         scratch_shapes=[
             pltpu.VMEM((2 * HALF + 4, ROWS, COLS), bf16),
@@ -362,7 +396,8 @@
             pltpu.VMEM((HALF, 2, 128, COLS), bf16),
             pltpu.VMEM((HALF, ROWS, COLS), bf16),
             pltpu.VMEM((4, ROWS, COLS), bf16),
-            pltpu.SemaphoreType.DMA((29,)),
+            pltpu.SMEM((2, 2 * HALF), jnp.int32),
+            pltpu.SemaphoreType.DMA((30,)),
             pltpu.SemaphoreType.DMA((26,)),
             pltpu.SemaphoreType.DMA((26,)),
             pltpu.SemaphoreType.DMA((2,)),
@@ -371,7 +406,7 @@
             pltpu.SemaphoreType.DMA((HALF,)),
             pltpu.SemaphoreType.DMA((HALF,)),
             pltpu.SemaphoreType.DMA((HALF,)),
-            pltpu.SemaphoreType.REGULAR((6,)),
+            pltpu.SemaphoreType.REGULAR((8,)),
         ],
         compiler_params=pltpu.CompilerParams(
             collective_id=0, has_side_effects=True, vmem_limit_bytes=58 << 20

time: 285 us -> 281 us (0.986)
  Pallas kernels: 282 us -> 279 us
    pallas_call x1, Pallas kernels: 282 us -> 279 us  [on_device(): pl.pallas_call(kernel, out_shape=pltpu.VMEM((boxes, ROWS, COLS), bf16), i...]
where the time goes in v3:
time: 281 us
  Pallas kernels  279 us (99%)
    pallas_call x1, Pallas kernels, on_device(): pl.pallas_call(kernel, out_shape=pltpu.VMEM((boxes, ROWS, COLS), bf16), i...  279 us

profile of v3, /device:TPU:30, one launch (start us, length us, event | category | flops | bytes accessed | tf_op | source)
XLA Modules:
  0.0 280.8 jit_solution(6603228048387790048)
XLA Ops:
  0.0 278.8 %butterfly.1 = bf16[64,128,256]{2,1,0:T(8,128)(2,1)S(1)} custom-call(bf16[64,128,256]{2,1,0:T(8,128)(2,1)} %bitcast.13, bf16[64,64,128]{2,1,0:T(8,128)(2,1)} %bitcast.15, bf16[64,64,128]{2,1,0:T(8,128)(2,1)} %bitcast.16, bf16[128,64,128]{2,1,0:T(8,128)(2,1)} %bitcast.14, s32[2,64]{1,0:T(2,128)} %bitcast.17, bf16[3,128,64,128]{3,2,1,0:T(8,128)(2,1)} %bitcast.11, ...), custom_call_target="tpu_custom_call" | custom-call | tf_op jit(solution)/shard_map/butterfly/pallas_call | solution.py:379
  278.8 2.0 copy.11

commit v4 on v3

--- a/solution.py
+++ b/solution.py
@@ -25,7 +25,7 @@
     out,
     x, x_other, w_in, w_out, w_near, w_edge, v_in, v_out, s_in, s_out, z, y, o, edge, offsets,
     load_sem, pair_send, pair_recv, halo_send, halo_recv, mix_send, mix_recv,
-    back_send, back_recv, known,
+    back_send, back_recv, known, hop, hop_sem,
 ):
     leaf = lax.axis_index("leaf")
     mine = lax.axis_index("rhs")
@@ -54,12 +54,12 @@
             device_id=device, device_id_type=MESH,
         )
 
-    def parts(step, owner, columns):
+    def parts(step, owner):
         g = (turn + step) % STEPS
         h = (turn + STEPS - step) % STEPS
         box, row_box = owner * HALF + GROUP * g, owner * HALF + GROUP * h
         return (
-            (rhs.at[pl.ds(box, 8)], columns(box, GROUP * g)),
+            (rhs.at[pl.ds(box, 8)], x_other.at[pl.ds(GROUP * g, 8)]),
             (basis_in.at[pl.ds(box, 8)], w_in.at[pl.ds(GROUP * g, 8), half_rows]),
             (
                 values_in.at[:, pl.ds(2 * box, 16)],
@@ -76,34 +76,44 @@
             ),
         )
 
-    def load(step, part):
-        src, dst = parts(step, mine, lambda box, at: x.at[pl.ds(2 + box, 8)])[part]
-        return pltpu.make_async_copy(src, dst, load_sem.at[6 * step + part])
-
-    def pair(step, part, owner=other):
-        src, dst = parts(step, owner, lambda box, at: x_other.at[pl.ds(at, 8)])[part]
-        at = 6 * step + part
-        return copy_to(src, dst, pair_send.at[at], pair_recv.at[at], partner)
+    def pair(step, part):
+        src, dst = parts(step, other)[part]
+        recv = pair_recv.at[step + STEPS * (part // 3)]
+        return copy_to(src, dst, pair_send.at[part], recv, partner)
+
+    def halves(box):
+        return (
+            (basis_in.at[pl.ds(box, HALF)], w_in.at[:, half_rows]),
+            (values_in.at[:, pl.ds(2 * box, 2 * HALF)], v_in.at[:, :, half_rows]),
+            (values_out.at[:, pl.ds(2 * box, 2 * HALF)], v_out.at[:, :, half_rows]),
+            (basis_out.at[pl.ds(box, HALF)], w_out.at[:, half_rows]),
+            (near.at[pl.ds(2 * box, 2 * HALF)], w_near.at[:, half_rows]),
+        )
+
+    def bulk(boxes, recv):
+        return copy_to(
+            rhs.at[pl.ds(0, boxes)], x_other.at[pl.ds(0, boxes)], pair_send.at[0], recv, partner
+        )
 
     def edges(at, owner):
         first = 2 * (HALF * owner + 30 * at)
         return near.at[pl.ds(first, 4)], w_edge.at[pl.ds(4 * at, 4), half_rows]
 
-    load_rest = [
-        pltpu.make_async_copy(*edges(at, other), load_sem.at[24 + at]) for at in range(2)
-    ] + [
-        pltpu.make_async_copy(
-            rhs.at[pl.ds(HALF * other, HALF)], x.at[pl.ds(2 + HALF * other, HALF)],
-            load_sem.at[26],
-        )
-    ]
-    load_scales = [
-        pltpu.make_async_copy(scales_in.at[:, pl.ds(16 * mine, 16)], s_in, load_sem.at[27]),
-        pltpu.make_async_copy(scales_out.at[:, pl.ds(16 * mine, 16)], s_out, load_sem.at[28]),
-        pltpu.make_async_copy(near_offsets, offsets, load_sem.at[29]),
+    loads = [
+        pltpu.make_async_copy(src, dst, load_sem.at[n])
+        for n, (src, dst) in enumerate(
+            ((rhs, x.at[pl.ds(2, 2 * HALF)]),)
+            + halves(HALF * mine)
+            + (edges(0, other), edges(1, other))
+            + (
+                (scales_in.at[:, pl.ds(16 * mine, 16)], s_in),
+                (scales_out.at[:, pl.ds(16 * mine, 16)], s_out),
+                (near_offsets, offsets),
+            )
+        )
     ]
     pair_edges = [
-        copy_to(*edges(at, mine), pair_send.at[24 + at], pair_recv.at[24 + at], partner)
+        copy_to(*edges(at, mine), pair_send.at[6], pair_recv.at[8], partner)
         for at in range(2)
     ]
     halo_up = copy_to(
@@ -115,9 +125,49 @@
         halo_send.at[1], halo_recv.at[1], (leaf - 1, mine),
     )
 
+    seam_up, seam_down = leaf == HALF - 1, leaf == HALF
+
+    def seam_first(n):
+        rows = pl.ds(32 * n, 32)
+        up = copy_to(
+            rhs.at[pl.ds(62, 2), rows], hop, halo_send.at[0], hop_sem.at[0],
+            (leaf - 6 + 2 * n, mine),
+        )
+        down = copy_to(
+            rhs.at[pl.ds(0, 2), rows], hop, halo_send.at[1], hop_sem.at[0],
+            (leaf + 2 * n, mine),
+        )
+        return up, down
+
+    def seam_last(n, src_up, src_down, send_up, send_down):
+        rows = pl.ds(32 * n, 32)
+        up = copy_to(
+            src_up, x.at[pl.ds(0, 2), rows], send_up, halo_recv.at[0], (HALF, mine)
+        )
+        down = copy_to(
+            src_down, x.at[pl.ds(66, 2), rows], send_down, halo_recv.at[1], (HALF - 1, mine)
+        )
+        return up, down
+
+    def seam_direct(n):
+        rows = pl.ds(32 * n, 32)
+        return seam_last(
+            n, rhs.at[pl.ds(62, 2), rows], rhs.at[pl.ds(0, 2), rows],
+            halo_send.at[0], halo_send.at[1],
+        )
+
+    def seam_relay(n):
+        return seam_last(n, hop, hop, hop_sem.at[1], hop_sem.at[1])
+
     def mix(j):
         return copy_to(
-            z.at[j], y.at[slot], mix_send.at[j], mix_recv.at[slot], (mine * HALF + j, side)
+            z.at[j], y.at[slot], mix_send.at[0], mix_recv.at[slot // GROUP],
+            (mine * HALF + j, side),
+        )
+
+    def mixed(boxes, recv):
+        return copy_to(
+            z.at[pl.ds(0, boxes)], y.at[pl.ds(0, boxes)], mix_send.at[0], recv, partner
         )
 
     def is_self(j):
@@ -126,14 +176,14 @@
     def on_edge(b):
         return (b < 2) | (b >= HALF - 2)
 
-    def back(b, owner=mine):
+    def back(b):
         return copy_to(
-            o.at[b], out.at[owner * HALF + b], back_send.at[b], back_recv.at[b], partner
+            o.at[b], out.at[mine * HALF + b], back_send.at[0], back_recv.at[0], partner
         )
 
     def back_edge(b):
         return copy_to(
-            o.at[b], edge.at[b % 28], back_send.at[b], back_recv.at[b], partner
+            o.at[b], edge.at[b % 28], back_send.at[0], back_recv.at[1], partner
         )
 
     barrier = pltpu.get_barrier_semaphore()
@@ -166,15 +216,7 @@
             pair(step, part).start()
     for copy in pair_edges:
         copy.start()
-    for step in range(STEPS):
-        for part in range(3):
-            load(step, part).start()
-    for copy in load_scales:
-        copy.start()
-    for step in range(STEPS):
-        for part in range(3, 6):
-            load(step, part).start()
-    for copy in load_rest:
+    for copy in loads:
         copy.start()
 
     @pl.when(lead)
@@ -201,14 +243,38 @@
     def _():
         pl.semaphore_wait(known.at[7], 1)
 
-    @pl.when(high)
+    @pl.when(high & jnp.logical_not(seam_up))
     def _():
         halo_up.start()
 
-    @pl.when(low)
+    @pl.when(low & jnp.logical_not(seam_down))
     def _():
         halo_down.start()
 
+    @pl.when(seam_up)
+    def _():
+        for n in range(3):
+            seam_first(n)[0].start()
+        seam_direct(3)[0].start()
+
+    @pl.when(seam_down)
+    def _():
+        for n in range(1, 4):
+            seam_first(n)[1].start()
+        seam_direct(0)[1].start()
+
+    for n in range(3):
+        @pl.when(leaf == HALF - 7 + 2 * n)
+        def _():
+            seam_first(n)[0].wait_recv()
+            seam_relay(n)[0].start()
+
+    for n in range(1, 4):
+        @pl.when(leaf == HALF + 2 * n)
+        def _():
+            seam_first(n)[1].wait_recv()
+            seam_relay(n)[1].start()
+
     @pl.when(jnp.logical_not(low))
     def _():
         x[0:2] = jnp.zeros((2, ROWS, COLS), jnp.bfloat16)
@@ -216,10 +282,6 @@
     @pl.when(jnp.logical_not(high))
     def _():
         x[66:68] = jnp.zeros((2, ROWS, COLS), jnp.bfloat16)
-
-    def arrived(step, part):
-        load(step, part).wait()
-        pair(step, part, mine).wait_recv()
 
     def levels(coeff, blocks, scales, g):
         for t in range(LEVELS):
@@ -243,14 +305,13 @@
                     coeff[i, c] = first.astype(jnp.bfloat16)
                     coeff[j, c] = second.astype(jnp.bfloat16)
 
-    for copy in load_scales:
+    for copy in loads:
         copy.wait()
 
     @pl.loop(0, STEPS)
     def _(step):
         g = (turn + step) % STEPS
-        for part in range(3):
-            arrived(step, part)
+        bulk(22, pair_recv.at[step]).wait_recv()
 
         @pl.loop(0, GROUP)
         def _(i):
@@ -272,9 +333,6 @@
             def _():
                 mix(j).start()
 
-    for copy in load_rest:
-        copy.wait()
-
     @pl.when(low)
     def _():
         halo_up.wait_recv()
@@ -286,18 +344,16 @@
     @pl.loop(0, STEPS)
     def _(step):
         h = (turn + STEPS - step) % STEPS
-        for part in range(3, 6):
-            arrived(step, part)
-
-        @pl.loop(0, GROUP)
-        def _(i):
-            d = GROUP * h + i
-
-            @pl.when(jnp.logical_not(is_self(d)))
-            def _():
-                copy_to(
-                    z.at[d], y.at[d], mix_send.at[d], mix_recv.at[d], partner
-                ).wait_recv()
+        bulk(18, pair_recv.at[STEPS + step]).wait_recv()
+        with_self = (side == mine) & (slot // GROUP == h)
+
+        @pl.when(with_self)
+        def _():
+            mixed(GROUP - 1, mix_recv.at[h]).wait_recv()
+
+        @pl.when(jnp.logical_not(with_self))
+        def _():
+            mixed(GROUP, mix_recv.at[h]).wait_recv()
 
         levels(y, v_out, s_out, h)
 
@@ -327,46 +383,55 @@
             )
             out[row] = dot(left, right, 0).astype(jnp.bfloat16)
 
-    for copy in pair_edges:
-        copy.wait_recv()
+    bulk(HALF, pair_recv.at[0]).wait_send()
+    for n, (src, dst) in enumerate(halves(0)):
+        copy_to(src, dst, pair_send.at[1 + n], pair_recv.at[0], partner).wait_send()
+    pair_edge = copy_to(
+        near.at[pl.ds(0, 8)], w_edge.at[:, half_rows], pair_send.at[6], pair_recv.at[8], partner
+    )
+    pair_edge.wait_send()
+
+    @pl.when(high)
+    def _():
+        halo_up.wait_send()
+
+    @pl.when(low)
+    def _():
+        halo_down.wait_send()
+
+    for n in range(3):
+        @pl.when((leaf == HALF - 7 + 2 * n) | (leaf == HALF + 2 * n + 2))
+        def _():
+            seam_relay(n)[0].wait_send()
+
+    @pl.when(side == mine)
+    def _():
+        mixed(HALF - 1, mix_recv.at[0]).wait_send()
+
+    @pl.when(side != mine)
+    def _():
+        mixed(HALF, mix_recv.at[0]).wait_send()
+
+    pair_edge.wait_recv()
+    copy_to(
+        o.at[pl.ds(0, 4)], edge, back_send.at[0], back_recv.at[1], partner
+    ).wait_recv()
 
     @pl.loop(0, 4)
     def _(e):
-        b = e + 28 * (e // 2)
-        row = HALF * other + b
+        row = HALF * other + e + 28 * (e // 2)
         left = jnp.concatenate([w_edge[2 * e], w_edge[2 * e + 1]], axis=0)
         right = jnp.concatenate(
             [x[2 + row + offsets[0, row]], x[2 + row + offsets[1, row]]], axis=0
         )
-        add = dot(left, right, 0)
-        back_edge(b).wait_recv()
-        out[row] = (edge[e].astype(jnp.float32) + add).astype(jnp.bfloat16)
-
-    for step in range(STEPS):
-        for part in range(6):
-            pair(step, part).wait_send()
-    for copy in pair_edges:
-        copy.wait_send()
-
-    @pl.when(high)
-    def _():
-        halo_up.wait_send()
-
-    @pl.when(low)
-    def _():
-        halo_down.wait_send()
-
-    @pl.loop(0, HALF)
-    def _(j):
-        @pl.when(jnp.logical_not(is_self(j)))
-        def _():
-            mix(j).wait_send()
-
-        back(j).wait_send()
-
-        @pl.when(jnp.logical_not(on_edge(j)))
-        def _():
-            back(j, other).wait_recv()
+        out[row] = (edge[e].astype(jnp.float32) + dot(left, right, 0)).astype(jnp.bfloat16)
+
+    copy_to(
+        o, out.at[pl.ds(0, HALF)], back_send.at[0], back_recv.at[0], partner
+    ).wait_send()
+    copy_to(
+        o.at[pl.ds(0, 28)], out.at[pl.ds(0, 28)], back_send.at[0], back_recv.at[0], partner
+    ).wait_recv()
 
 
 def on_device(
@@ -397,16 +462,18 @@
             pltpu.VMEM((HALF, ROWS, COLS), bf16),
             pltpu.VMEM((4, ROWS, COLS), bf16),
             pltpu.SMEM((2, 2 * HALF), jnp.int32),
-            pltpu.SemaphoreType.DMA((30,)),
-            pltpu.SemaphoreType.DMA((26,)),
-            pltpu.SemaphoreType.DMA((26,)),
+            pltpu.SemaphoreType.DMA((11,)),
+            pltpu.SemaphoreType.DMA((7,)),
+            pltpu.SemaphoreType.DMA((9,)),
             pltpu.SemaphoreType.DMA((2,)),
             pltpu.SemaphoreType.DMA((2,)),
-            pltpu.SemaphoreType.DMA((HALF,)),
-            pltpu.SemaphoreType.DMA((HALF,)),
-            pltpu.SemaphoreType.DMA((HALF,)),
-            pltpu.SemaphoreType.DMA((HALF,)),
+            pltpu.SemaphoreType.DMA((1,)),
+            pltpu.SemaphoreType.DMA((STEPS,)),
+            pltpu.SemaphoreType.DMA((1,)),
+            pltpu.SemaphoreType.DMA((2,)),
             pltpu.SemaphoreType.REGULAR((8,)),
+            pltpu.VMEM((2, 32, COLS), bf16),
+            pltpu.SemaphoreType.DMA((2,)),
         ],
         compiler_params=pltpu.CompilerParams(
             collective_id=0, has_side_effects=True, vmem_limit_bytes=58 << 20

time: 281 us -> 278 us (0.989)
  Pallas kernels: 279 us -> 276 us
    pallas_call x1, Pallas kernels: 279 us -> 276 us  [on_device(): pl.pallas_call(kernel, out_shape=pltpu.VMEM((boxes, ROWS, COLS), bf16), i...]
where the time goes in v4:
time: 278 us
  Pallas kernels  276 us (99%)
    pallas_call x1, Pallas kernels, on_device(): pl.pallas_call(kernel, out_shape=pltpu.VMEM((boxes, ROWS, COLS), bf16), i...  276 us

profile of v4, /device:TPU:30, one launch (start us, length us, event | category | flops | bytes accessed | tf_op | source)
XLA Modules:
  0.0 277.9 jit_solution(17246382437110007252)
XLA Ops:
  0.0 275.9 %butterfly.1 = bf16[64,128,256]{2,1,0:T(8,128)(2,1)S(1)} custom-call(bf16[64,128,256]{2,1,0:T(8,128)(2,1)} %bitcast.13, bf16[64,64,128]{2,1,0:T(8,128)(2,1)} %bitcast.15, bf16[64,64,128]{2,1,0:T(8,128)(2,1)} %bitcast.16, bf16[128,64,128]{2,1,0:T(8,128)(2,1)} %bitcast.14, s32[2,64]{1,0:T(2,128)} %bitcast.17, bf16[3,128,64,128]{3,2,1,0:T(8,128)(2,1)} %bitcast.11, ...), custom_call_target="tpu_custom_call" | custom-call | tf_op jit(solution)/shard_map/butterfly/pallas_call | solution.py:444
  275.9 2.0 copy.11

commit v5 on v4

--- a/solution.py
+++ b/solution.py
@@ -81,6 +81,17 @@
         recv = pair_recv.at[step + STEPS * (part // 3)]
         return copy_to(src, dst, pair_send.at[part], recv, partner)
 
+    def start_pair(step, part):
+        src, dst = parts(step, other)[part]
+        recv = pair_recv.at[step + STEPS * (part // 3)]
+        if part in (2, 3):
+            cuts = [(t, pl.ds(4 * n, 4)) for t in range(LEVELS) for n in range(4)]
+        else:
+            size = {0: 1, 1: 4, 4: 4, 5: 4}[part]
+            cuts = [(pl.ds(size * n, size),) for n in range(src.shape[0] // size)]
+        for at in cuts:
+            copy_to(src.at[at], dst.at[at], pair_send.at[part], recv, partner).start()
+
     def halves(box):
         return (
             (basis_in.at[pl.ds(box, HALF)], w_in.at[:, half_rows]),
@@ -210,10 +221,10 @@
 
     for step in range(STEPS):
         for part in range(3):
-            pair(step, part).start()
+            start_pair(step, part)
     for step in range(STEPS):
         for part in range(3, 6):
-            pair(step, part).start()
+            start_pair(step, part)
     for copy in pair_edges:
         copy.start()
     for copy in loads:

time: 278 us -> 278 us (level)
  no operation moved by 1% of the time
where the time goes in v5:
time: 278 us
  Pallas kernels  276 us (99%)
    pallas_call x1, Pallas kernels, on_device(): pl.pallas_call(kernel, out_shape=pltpu.VMEM((boxes, ROWS, COLS), bf16), i...  276 us

profile of v5, /device:TPU:30, one launch (start us, length us, event | category | flops | bytes accessed | tf_op | source)
XLA Modules:
  0.0 277.9 jit_solution(10492190758090025271)
XLA Ops:
  0.0 275.9 %butterfly.1 = bf16[64,128,256]{2,1,0:T(8,128)(2,1)S(1)} custom-call(bf16[64,128,256]{2,1,0:T(8,128)(2,1)} %bitcast.13, bf16[64,64,128]{2,1,0:T(8,128)(2,1)} %bitcast.15, bf16[64,64,128]{2,1,0:T(8,128)(2,1)} %bitcast.16, bf16[128,64,128]{2,1,0:T(8,128)(2,1)} %bitcast.14, s32[2,64]{1,0:T(2,128)} %bitcast.17, bf16[3,128,64,128]{3,2,1,0:T(8,128)(2,1)} %bitcast.11, ...), custom_call_target="tpu_custom_call" | custom-call | tf_op jit(solution)/shard_map/butterfly/pallas_call | solution.py:455
  275.9 2.0 copy.11
